TPU v7x, 128 devices: a whole 4x4x4 slice. The times are simulated.
128 devices in a mesh: row: 16 (over z, x_lo, core), col: 8 (over x_hi, y).
Axes of the slice: x: 4 (x_hi: 2, x_lo: 2; x = x_hi * 2 + x_lo), y: 4, z: 4, core: 2. Of those that a mesh axis runs over, the one named last changes fastest.
Arguments:
- base_weight: bfloat16 [16384, 49152], P('row', 'col'), may hold values from -6 to 6
- left_factor: float32 [16384, 256], P('row', 'col'), may hold values from -6 to 6
- right_factor: float32 [256, 49152], P('row', 'col'), may hold values from -0.375 to 0.375
Outputs:
- merged: bfloat16 [16384, 49152], P(None, ('row', 'col'))
All inputs are finite; a program needn't handle non-finite values.
Results may differ from a plain program's by a relative error of at most 0.001.
Values may be sent and summed in bfloat16 or wider, within the bound.
No kernel may reach another device: no remote copies, remote signals or barrier semaphores. Data moves between devices by JAX's collectives and lax.ppermute only.
A program may use at most 192 MiB of HBM per device.

v0:
```python
import jax
import jax.numpy as jnp
from jax import lax
from jax.sharding import PartitionSpec as P


def copy_for_each(value, axis):
    length = lax.axis_size(axis)
    return lax.all_to_all(
        jnp.broadcast_to(value[None], (length, *value.shape)), axis, 0, 0, tiled=True
    )


def joined_along(tiles, dim):
    tiles = jnp.moveaxis(tiles, 0, dim)
    lengths = tiles.shape
    return tiles.reshape(*lengths[:dim], lengths[dim] * lengths[dim + 1], *lengths[dim + 2 :])


def gathered_copies(value, axis, dim):
    tiles = copy_for_each(value, axis)
    return joined_along(tiles, dim)


def to_serving(stored):
    row_count = lax.axis_size("row")
    col_count = lax.axis_size("col")
    height = stored.shape[0]
    block_width = stored.shape[1] // row_count
    group_count = row_count // col_count
    shaped = stored.reshape(height, group_count, col_count, block_width)
    across = lax.all_to_all(shaped, "col", split_axis=2, concat_axis=1, tiled=True)
    served = lax.all_to_all(across, "row", split_axis=1, concat_axis=0, tiled=True)
    return served.reshape(height * row_count, block_width)


def body(base_weight, left_factor, right_factor):
    left_cols = gathered_copies(left_factor, "col", 1)
    delta = jnp.dot(
        left_cols,
        lax.all_gather(right_factor, "row", axis=0, tiled=True),
        precision=lax.Precision.HIGHEST,
        preferred_element_type=jnp.float32,
    )
    merged_block = (base_weight.astype(jnp.float32) + delta).astype(jnp.bfloat16)
    return to_serving(merged_block)


def solution(mesh):
    placed = (P("row", "col"), P("row", "col"), P("row", "col"))
    return jax.shard_map(
        body, mesh=mesh, in_specs=placed, out_specs=P(None, ("row", "col")), check_vma=False
    )
```

profile of v0, /device:TPU:1, one launch (start us, length us, event | category | flops | bytes accessed | tf_op | source)
XLA Modules:
  0.0 399.2 jit_solution(9621992016833128022)
XLA Ops:
  6.5 0.0 all-gather.2.cloned.1.call-start
  6.5 0.7 all-gather.2.cloned.1.call-update
  7.3 1.0 broadcast_in_dim.2
  8.3 26.6 %all_to_all.38 = f32[8,1024,32]{1,2,0:T(8,128)S(1)} all-to-all(f32[8,1024,32]{1,2,0:T(8,128)S(1)} %broadcast_in_dim.2), channel_id=1, replica_groups=mesh['row'=16,'col'=8] {'col'}, dimensions={0} | all-to-all | bytes 2097152 | tf_op jit(solution)/shard_map/all_to_all | solution.py:9
  34.9 25.6 %all-gather.2.cloned.1.call-done = f32[256,6144]{1,0:T(8,128)} async-done(((f32[16,6144]{1,0:T(8,128)}), f32[256,6144]{1,0:T(8,128)}) %all-gather.2.cloned.1.call-update) | async-done | bytes 6291472 | tf_op jit(solution)/shard_map/all_gather | solution.py:41
  60.4 23.9 %add_convert_fusion = bf16[1024,6144]{1,0:T(8,128)(2,1)S(1)} fusion(bf16[1024,6144]{1,0:T(8,128)(2,1)} %param.3, f32[1024,256]{0,1:T(8,128)S(1)} %bitcast.24, f32[256,6144]{1,0:T(8,128)} %all-gather.2.cloned.1.call-done), kind=kOutput, calls=%fused_computation | convolution fusion | flops 19346227200 | bytes 32505856 | tf_op jit(solution)/shard_map/dot_general | solution.py:39
  84.3 3.0 copy.8
  87.3 7.9 %copy.6 = bf16[1024,2,8,384]{3,0,1,2:T(8,128)(2,1)S(1)} copy(bf16[1024,2,8,384]{3,2,1,0:T(8,128)(2,1)S(1)} %bitcast.21) | data formatting | bytes 25165824 | tf_op jit(solution)/shard_map/reshape | solution.py:31
  95.2 146.6 %all_to_all.39 = bf16[1024,2,8,384]{3,0,1,2:T(8,128)(2,1)S(1)} all-to-all(bf16[1024,2,8,384]{3,0,1,2:T(8,128)(2,1)S(1)} %copy.6), channel_id=1, replica_groups=mesh['row'=16,'col'=8] {'col'}, dimensions={2} | all-to-all | bytes 25165824 | tf_op jit(solution)/shard_map/all_to_all | solution.py:32
  241.9 145.6 %all_to_all.40 = bf16[1024,16,1,384]{3,0,2,1:T(8,128)(2,1)S(1)} all-to-all(bf16[1024,16,1,384]{3,0,2,1:T(8,128)(2,1)S(1)} %bitcast.22), channel_id=1, replica_groups=mesh['row'=16,'col'=8] {'row'}, dimensions={1} | all-to-all | bytes 25165824 | tf_op jit(solution)/shard_map/all_to_all | solution.py:33
  387.5 4.8 %copy.10 = bf16[16384,384]{1,0:T(8,128)(2,1)} copy(bf16[16384,384]{1,0:T(8,128)(2,1)S(1)} %bitcast.23) | data formatting | bytes 25165824
Async XLA Ops:
  6.5 53.9 %all-gather.2.cloned.1.call-start = ((), (), s32[]{:S(2)}) async-start(), calls=%async_computation.3 | async-start | bytes 6684672 | tf_op jit(solution)/shard_map/all_gather | solution.py:41
Sparse Core Ops, SparseCore 0:
  9.1 51.3 all-gather.1
where the time goes:
time: 399 us
  blocking collectives  319 us (80%)
  waiting for transfers between devices  26.3 us (7%)
  matrix products  23.9 us (6%)
  local copies, waits for them, and re-layouts  16.7 us (4%)
  between operations  13.4 us (3%)
    all_to_all x1, blocking collectives, to_serving(): lax.all_to_all(shaped, 'col', split_axis=2, concat_axis=1, tiled=True)  147 us
    all_to_all x1, blocking collectives, to_serving(): lax.all_to_all(across, 'row', split_axis=1, concat_axis=0, tiled=True)  146 us
    all_to_all x1, blocking collectives, copy_for_each(): lax.all_to_all(jnp.broadcast_to(value[None], (length, *value.shape)), axi...  26.6 us
    all_gather x1, waiting for transfers between devices, body(): lax.all_gather(right_factor, 'row', axis=0, tiled=True)  25.6 us
    dot_general x1, matrix products, body(): jnp.dot(left_cols, lax.all_gather(right_factor, 'row', axis=0, tiled=True...  23.9 us
  transfers between devices with their start and end apart: 1, of which 1 were waited for; matrix products, arithmetic and copies ran while one was open for 0% of the time, Pallas kernels for 0%

commit v1 on v0

--- a/solution.py
+++ b/solution.py
@@ -38,7 +38,12 @@
     left_cols = gathered_copies(left_factor, "col", 1)
     delta = jnp.dot(
         left_cols,
-        lax.all_gather(right_factor, "row", axis=0, tiled=True),
+        jnp.concatenate(
+            jax.lax.all_to_all(
+                jnp.stack(jax.lax.psum(1, "row") * [right_factor], axis=0), "row", 0, 0
+            ),
+            axis=0,
+        ),
         precision=lax.Precision.HIGHEST,
         preferred_element_type=jnp.float32,
     )

time: 399 us -> 432 us (1.083)
  blocking collectives: 319 us -> 389 us
  waiting for transfers between devices: 26.3 us -> 0 us
  between operations: 13.4 us -> 0.04 us
    all_to_all x0 -> x1, blocking collectives: none -> 79.3 us  [body(): jax.lax.all_to_all(jnp.stack(jax.lax.psum(1, 'row') * [right_factor], axi...]
    all_gather x1 -> x0, waiting for transfers between devices: 25.6 us -> none  [body(): lax.all_gather(right_factor, 'row', axis=0, tiled=True)]
    all_to_all x1, blocking collectives: 147 us -> 141 us  [to_serving(): lax.all_to_all(shaped, 'col', split_axis=2, concat_axis=1, tiled=True)]
  transfers between devices with their start and end apart: 1 -> 0, of which waited for: 1 -> 0; matrix products, arithmetic and copies ran while one was open for 0% -> 0% of each run, Pallas kernels for 0% -> 0%
where the time goes in v1:
time: 432 us; the launch traced here: 431 us
  blocking collectives  389 us (90%)
  matrix products  23.9 us (6%)
  local copies, waits for them, and re-layouts  18.4 us (4%)
    all_to_all x1, blocking collectives, to_serving(): lax.all_to_all(across, 'row', split_axis=1, concat_axis=0, tiled=True)  146 us
    all_to_all x1, blocking collectives, to_serving(): lax.all_to_all(shaped, 'col', split_axis=2, concat_axis=1, tiled=True)  141 us
    all_to_all x1, blocking collectives, body(): jax.lax.all_to_all(jnp.stack(jax.lax.psum(1, 'row') * [right_factor], axi...  79.3 us
    dot_general x1, matrix products, body(): jnp.dot(left_cols, jnp.concatenate(jax.lax.all_to_all(jnp.stack(jax.lax.p...  23.9 us
    all_to_all x1, blocking collectives, copy_for_each(): lax.all_to_all(jnp.broadcast_to(value[None], (length, *value.shape)), axi...  22.9 us

profile of v1, /device:TPU:1, one launch (start us, length us, event | category | flops | bytes accessed | tf_op | source)
XLA Modules:
  0.0 431.4 jit_solution(8993340598130317654)
XLA Ops:
  0.0 1.0 broadcast_in_dim.2
  1.0 22.9 %all_to_all.43 = f32[8,1024,32]{1,2,0:T(8,128)S(1)} all-to-all(f32[8,1024,32]{1,2,0:T(8,128)S(1)} %broadcast_in_dim.2), channel_id=1, replica_groups=mesh['row'=16,'col'=8] {'col'}, dimensions={0} | all-to-all | bytes 2097152 | tf_op jit(solution)/shard_map/all_to_all | solution.py:9
  23.9 1.7 stack.2
  25.6 79.3 %all_to_all.44 = f32[16,16,6144]{2,1,0:T(8,128)S(1)} all-to-all(f32[16,16,6144]{2,1,0:T(8,128)S(1)} %stack.2), channel_id=1, replica_groups=mesh['row'=16,'col'=8] {'row'}, dimensions={0} | all-to-all | bytes 12582912 | tf_op jit(solution)/shard_map/all_to_all | solution.py:42
  104.9 23.9 %add_convert_fusion = bf16[1024,6144]{1,0:T(8,128)(2,1)S(1)} fusion(bf16[1024,6144]{1,0:T(8,128)(2,1)} %param.3, f32[1024,256]{0,1:T(8,128)S(1)} %bitcast.26, f32[256,6144]{1,0:T(8,128)S(1)} %bitcast.25), kind=kOutput, calls=%fused_computation | convolution fusion | flops 19346227200 | bytes 32505856 | tf_op jit(solution)/shard_map/dot_general | solution.py:39
  128.8 3.0 copy.8
  131.8 7.9 %copy.6 = bf16[1024,2,8,384]{3,0,1,2:T(8,128)(2,1)S(1)} copy(bf16[1024,2,8,384]{3,2,1,0:T(8,128)(2,1)S(1)} %bitcast.22) | data formatting | bytes 25165824 | tf_op jit(solution)/shard_map/reshape | solution.py:31
  139.7 141.2 %all_to_all.45 = bf16[1024,2,8,384]{3,0,1,2:T(8,128)(2,1)S(1)} all-to-all(bf16[1024,2,8,384]{3,0,1,2:T(8,128)(2,1)S(1)} %copy.6), channel_id=1, replica_groups=mesh['row'=16,'col'=8] {'col'}, dimensions={2} | all-to-all | bytes 25165824 | tf_op jit(solution)/shard_map/all_to_all | solution.py:32
  280.9 145.7 %all_to_all.46 = bf16[1024,16,1,384]{3,0,2,1:T(8,128)(2,1)S(1)} all-to-all(bf16[1024,16,1,384]{3,0,2,1:T(8,128)(2,1)S(1)} %bitcast.23), channel_id=1, replica_groups=mesh['row'=16,'col'=8] {'row'}, dimensions={1} | all-to-all | bytes 25165824 | tf_op jit(solution)/shard_map/all_to_all | solution.py:33
  426.6 4.8 %copy.10 = bf16[16384,384]{1,0:T(8,128)(2,1)} copy(bf16[16384,384]{1,0:T(8,128)(2,1)S(1)} %bitcast.24) | data formatting | bytes 25165824
